TPU v7x, 512 devices: a whole 4x4x16 slice. The times are simulated.
512 devices in a mesh: src: 64 (over z_hi, y, x, core), fac: 8 (over z_lo).
Axes of the slice: x: 4, y: 4, z: 16 (z_hi: 2, z_lo: 8; z = z_hi * 8 + z_lo), core: 2. Of those that a mesh axis runs over, the one named last changes fastest.
Arguments:
- lower_inverse: bfloat16 [8, 1024, 2, 1024], P('fac', 'src'), as said below
- coupling: bfloat16 [8, 1024, 2, 1024], P('fac', 'src'), as said below
- source_cell: int32 [8192], P('src'), may hold values from 0 to 8191
- source_wave: float32 [8192, 2], P('src'), may hold values from -6 to 6
- inflow_field: bfloat16 [8192, 2, 1024], P('src'), may hold values from -6 to 6
- receiver_cell: int32 [8192, 128], P('src'), may hold values from 0 to 8191
- observed: float32 [8192, 2, 128], P('src'), may hold values from -6 to 6
- adjoint: bfloat16 [8192, 8, 2, 1024], P('src', 'fac'), may hold values from -16 to 16
Outputs:
- wavefield: float32 [8192, 8, 2, 1024], P('src', 'fac')
- data_residual: float32 [8192, 2, 128], P('src')
- gradient: float32 [8, 1024], P('fac', 'src')
Inputs may be any that keep to these rules, and one draw needn't show every extreme that they name: lower_inverse[i, j, p, k] is zero where k > j. coupling[i, j, p, k] is zero where k < j.
All inputs are finite; a program needn't handle non-finite values.
Results may differ from a plain program's by a relative error of at most 0.025.
Values may be sent and summed in bfloat16 or wider, within the bound.
No kernel may reach another device: no remote copies, remote signals or barrier semaphores. Data moves between devices by JAX's collectives and lax.ppermute only.
A program may use at most 64 MiB of HBM per device.

v0:
```python
import math
import jax
import jax.numpy as jnp
from jax import lax
from jax.sharding import PartitionSpec as P


def from_behind(shard, axis, by):
    size = lax.axis_size(axis)
    pairs = [(i, i + by) for i in range(size) if 0 <= i + by < size]
    return lax.ppermute(shard, axis, pairs)


def complex_apply(vector, matrix):
    width = matrix.shape[0]
    joined = matrix.reshape(width, 2 * width)
    real_row = jnp.concatenate([vector[:, 0], -vector[:, 1]], axis=1)
    imag_row = jnp.concatenate([vector[:, 1], vector[:, 0]], axis=1)
    stacked = jnp.stack([real_row, imag_row], axis=1).reshape(-1, 2 * width)
    contract_dims = (((1,), (1,)), ((), ()))
    result = lax.dot_general(stacked, joined, contract_dims, preferred_element_type=jnp.float32)
    return result.reshape(vector.shape[0], 2, width)


def source_block(cells, wave, owner, width):
    cell_ids = owner * width + lax.broadcasted_iota(jnp.int32, (width,), 0)
    hit = cells[:, None] == cell_ids[None, :]
    return jnp.where(hit[:, None, :], wave[:, :, None], jnp.zeros((), jnp.float32))


def block_solve(previous, cells, wave, owner, lower_full, coupling_full):
    width = lower_full.shape[0]
    term = source_block(cells, wave, owner, width)
    reduced = (term - complex_apply(previous, coupling_full)).astype(jnp.bfloat16)
    return complex_apply(reduced, lower_full)


def per_device(
    lower_inverse,
    coupling,
    source_cell,
    source_wave,
    inflow_field,
    receiver_cell,
    observed,
    adjoint,
):
    owner = lax.axis_index("fac")
    fac_count = lax.axis_size("fac")
    width = lower_inverse.shape[3]
    sources = source_cell.shape[0]
    whole_lower, whole_coupling = (
        lax.all_gather(lower_inverse, "src", axis=1, tiled=True),
        lax.all_gather(coupling, "src", axis=1, tiled=True),
    )
    lower_full = whole_lower[0]
    coupling_full = whole_coupling[0]
    empty_field = jnp.zeros((sources, 2, width), jnp.float32)

    def section_step(section, carry):
        current, received = carry

        def compute():
            return block_solve(received, source_cell, source_wave, owner, lower_full, coupling_full)

        def unchanged():
            return current

        current = lax.cond(section == owner, compute, unchanged)
        received = from_behind(current.astype(jnp.bfloat16), "fac", 1)
        return (current, received)

    current, received = lax.fori_loop(0, fac_count, section_step, (empty_field, inflow_field))
    local_ids = receiver_cell - owner * width
    inside = (local_ids >= 0) & (local_ids < width)
    clipped = jnp.clip(local_ids, 0, width - 1)
    index_both = jnp.broadcast_to(clipped[:, None, :], observed.shape)
    values = jnp.take_along_axis(current, index_both, axis=2)
    values = jnp.where(inside[:, None, :], values, jnp.zeros((), jnp.float32))
    picked = lax.psum(values.astype(jnp.bfloat16), "fac").astype(jnp.float32)
    scale = 1.0 / math.sqrt(sources * lax.axis_size("src"))
    terms = jnp.sum(current * adjoint[:, 0].astype(jnp.float32), axis=(0, 1)) * scale
    gradient = lax.psum_scatter(terms[None, :], "src", scatter_dimension=1, tiled=True)
    return (current[:, None], picked - observed, gradient)


def solution(mesh):
    placed = (
        P("fac", "src", None, None),
        P("fac", "src", None, None),
        P("src"),
        P("src", None),
        P("src", None, None),
        P("src", None),
        P("src", None, None),
        P("src", "fac", None, None),
    )
    return jax.shard_map(
        per_device,
        mesh=mesh,
        in_specs=placed,
        out_specs=(P("src", "fac", None, None), P("src", None, None), P("fac", "src")),
        check_vma=False,
    )
```

profile of v0, /device:TPU:2, one launch (start us, length us, event | category | flops | bytes accessed | tf_op | source)
XLA Modules:
  0.0 1569.2 jit_solution(6800192813153071421)
XLA Ops:
  11.8 137.0 %all-gather.5.cloned.1.call-done = bf16[1,1024,2,1024]{3,2,0,1:T(2,128)(2,1)} async-done(((bf16[1,16,2,1024]{3,2,0,1:T(2,128)(2,1)}), bf16[1,1024,2,1024]{3,2,0,1:T(2,128)(2,1)}) %all-gather.5.cloned.1.call-update) | async-done | bytes 4194320 | tf_op jit(solution)/shard_map/all_gather | solution.py:53
  148.8 127.0 %all-gather.3.cloned.1.call-done = bf16[1,1024,2,1024]{3,2,0,1:T(2,128)(2,1)} async-done(((bf16[1,16,2,1024]{3,2,0,1:T(2,128)(2,1)}), bf16[1,1024,2,1024]{3,2,0,1:T(2,128)(2,1)}) %all-gather.3.cloned.1.call-update) | async-done | bytes 4194320 | tf_op jit(solution)/shard_map/all_gather | solution.py:54
  275.9 221.2 %while.18 = (s32[]{:T(128)}, f32[128,2,1024]{2,0,1:T(8,128)S(1)}, bf16[128,2,1024]{2,0,1:T(8,128)(2,1)S(1)}, s32[]{:T(128)}, s32[128]{0:T(128)}, /*index=5*/f32[...) while((s32[]{:T(128)}, f32[128,2,1024]{2,0,1:T(8,128)S(1)}, ...), condition=%wide.region_3.4_spmd, body=%wide.region_0.3_spmd.sunk | while | flops 2154169344 | bytes 39597816 | solution.py:73
  275.9 23.8 %conditional.2 = (f32[128,2,1024]{2,0,1:T(8,128)S(1)}) conditional(s32[]{:T(128)} %convert_element_type.39, f32[128,2,1024]{2,0,1:T(8,128)S(1)} %get-tuple-element.280, (s32[128]{0:T(128)}, s32[]{:T(128)}, f32[128,2]{0,1:T(2,128)}, bf16[128,2,1024]{2,0,1:T(8,128)(2,1)S(1)}, bf16[1,1024,2,1024]{3,2,1,0:T(2,128)(2,1)}, ...), branch_computations={%region_1.0_spmd, %region_2.2_spmd} | conditional | flops 2153907200 | bytes 35927604 | solution.py:69
  277.0 7.8 reshape.71
  288.4 7.8 reshape.72
  301.1 11.8 collective-permute-done
  313.1 28.2 %collective-permute-start = (bf16[128,2,1024]{2,0,1:T(8,128)(2,1)S(1)}, bf16[128,2,1024]{2,0,1:T(8,128)(2,1)S(1)}, u32[]{:S(2)}, u32[]{:S(2)}) collective-permute-start(bf16[128,2,1024]{2,0,1:T(8,128)(2,1)S(1)} %convert_element_type.40), channel_id=1, source_target_pairs={{0,1},{1,2},{2,3},{3,4},{4,5},{5,6},{6,7},{8,9},{9,10},{10,11},{11... | collective-permute-start | bytes 1572872 | tf_op jit(solution)/shard_map/while/body/eval_jaxpr/ppermute | solution.py:11
  341.3 11.1 collective-permute-done
  352.4 4.4 collective-permute-start
  356.8 10.2 collective-permute-done
  367.1 26.3 %collective-permute-start = (bf16[128,2,1024]{2,0,1:T(8,128)(2,1)S(1)}, bf16[128,2,1024]{2,0,1:T(8,128)(2,1)S(1)}, u32[]{:S(2)}, u32[]{:S(2)}) collective-permute-start(bf16[128,2,1024]{2,0,1:T(8,128)(2,1)S(1)} %convert_element_type.40), channel_id=1, source_target_pairs={{0,1},{1,2},{2,3},{3,4},{4,5},{5,6},{6,7},{8,9},{9,10},{10,11},{11... | collective-permute-start | bytes 1572872 | tf_op jit(solution)/shard_map/while/body/eval_jaxpr/ppermute | solution.py:11
  393.4 9.6 collective-permute-done
  403.0 4.4 collective-permute-start
  407.5 8.6 collective-permute-done
  416.2 26.6 %collective-permute-start = (bf16[128,2,1024]{2,0,1:T(8,128)(2,1)S(1)}, bf16[128,2,1024]{2,0,1:T(8,128)(2,1)S(1)}, u32[]{:S(2)}, u32[]{:S(2)}) collective-permute-start(bf16[128,2,1024]{2,0,1:T(8,128)(2,1)S(1)} %convert_element_type.40), channel_id=1, source_target_pairs={{0,1},{1,2},{2,3},{3,4},{4,5},{5,6},{6,7},{8,9},{9,10},{10,11},{11... | collective-permute-start | bytes 1572872 | tf_op jit(solution)/shard_map/while/body/eval_jaxpr/ppermute | solution.py:11
  442.7 8.0 collective-permute-done
  450.8 4.4 collective-permute-start
  455.3 7.1 collective-permute-done
  462.4 28.0 %collective-permute-start = (bf16[128,2,1024]{2,0,1:T(8,128)(2,1)S(1)}, bf16[128,2,1024]{2,0,1:T(8,128)(2,1)S(1)}, u32[]{:S(2)}, u32[]{:S(2)}) collective-permute-start(bf16[128,2,1024]{2,0,1:T(8,128)(2,1)S(1)} %convert_element_type.40), channel_id=1, source_target_pairs={{0,1},{1,2},{2,3},{3,4},{4,5},{5,6},{6,7},{8,9},{9,10},{10,11},{11... | collective-permute-start | bytes 1572872 | tf_op jit(solution)/shard_map/while/body/eval_jaxpr/ppermute | solution.py:11
  490.5 6.6 collective-permute-done
  497.1 310.7 %gather_fusion = bf16[32768]{0:T(1024)(128)(2,1)S(1)} fusion(f32[128,2,1024]{2,0,1:T(8,128)S(1)} %get-tuple-element.168, s32[32768]{0:T(1024)S(1)} %bitcast.40), kind=kCustom, calls=%fused_computation | custom fusion | bytes 524288 | tf_op jit(solution)/shard_map/jit(take_along_axis)/gather | solution.py:78
  811.8 624.0 %reduce-scatter.4.cloned.1.call-done = f32[16,1]{1,0:T(8,128)} async-done(((f32[1024,1]{1,0:T(8,128)}), f32[16,1]{1,0:T(8,128)}) %reduce-scatter.4.cloned.1.call-update) | async-done | bytes 80
  1437.1 124.1 %all-reduce.2.cloned.1.call-done = bf16[128,2,128]{2,1,0:T(2,128)(2,1)} async-done(((bf16[128,2,128]{2,1,0:T(2,128)(2,1)}), bf16[128,2,128]{2,1,0:T(2,128)(2,1)}) %all-reduce.2.cloned.1.call-update) | async-done | bytes 65552 | tf_op jit(solution)/shard_map/psum | solution.py:80
  (52 shorter events, 21.3 us)
Async XLA Ops:
  7.2 141.7 %all-gather.5.cloned.1.call-start = ((), (), s32[]{:S(2)}) async-start(), calls=%async_computation.2 | async-start | bytes 4259840 | tf_op jit(solution)/shard_map/all_gather | solution.py:53
  7.9 267.9 %all-gather.3.cloned.1.call-start = ((), (), s32[]{:S(2)}) async-start(), calls=%async_computation.1 | async-start | bytes 4259840 | tf_op jit(solution)/shard_map/all_gather | solution.py:54
  8.6 1427.2 %reduce-scatter.4.cloned.1.call-start = ((), (), s32[]{:S(2)}) async-start(), calls=%async_computation.4 | async-start | bytes 532480
  276.9 7.8 copy-start.2
  299.8 13.2 collective-permute-start
  313.1 39.2 %collective-permute-start = (bf16[128,2,1024]{2,0,1:T(8,128)(2,1)S(1)}, bf16[128,2,1024]{2,0,1:T(8,128)(2,1)S(1)}, u32[]{:S(2)}, u32[]{:S(2)}) collective-permute-start(bf16[128,2,1024]{2,0,1:T(8,128)(2,1)S(1)} %convert_element_type.40), channel_id=1, source_target_pairs={{0,1},{1,2},{2,3},{3,4},{4,5},{5,6},{6,7},{8,9},{9,10},{10,11},{11... | collective-permute-start | bytes 1572872 | tf_op jit(solution)/shard_map/while/body/eval_jaxpr/ppermute | solution.py:11
  352.4 14.6 collective-permute-start
  367.1 35.9 %collective-permute-start = (bf16[128,2,1024]{2,0,1:T(8,128)(2,1)S(1)}, bf16[128,2,1024]{2,0,1:T(8,128)(2,1)S(1)}, u32[]{:S(2)}, u32[]{:S(2)}) collective-permute-start(bf16[128,2,1024]{2,0,1:T(8,128)(2,1)S(1)} %convert_element_type.40), channel_id=1, source_target_pairs={{0,1},{1,2},{2,3},{3,4},{4,5},{5,6},{6,7},{8,9},{9,10},{10,11},{11... | collective-permute-start | bytes 1572872 | tf_op jit(solution)/shard_map/while/body/eval_jaxpr/ppermute | solution.py:11
  403.0 13.1 collective-permute-start
  416.2 34.6 %collective-permute-start = (bf16[128,2,1024]{2,0,1:T(8,128)(2,1)S(1)}, bf16[128,2,1024]{2,0,1:T(8,128)(2,1)S(1)}, u32[]{:S(2)}, u32[]{:S(2)}) collective-permute-start(bf16[128,2,1024]{2,0,1:T(8,128)(2,1)S(1)} %convert_element_type.40), channel_id=1, source_target_pairs={{0,1},{1,2},{2,3},{3,4},{4,5},{5,6},{6,7},{8,9},{9,10},{10,11},{11... | collective-permute-start | bytes 1572872 | tf_op jit(solution)/shard_map/while/body/eval_jaxpr/ppermute | solution.py:11
  450.8 11.5 collective-permute-start
  462.4 34.7 %collective-permute-start = (bf16[128,2,1024]{2,0,1:T(8,128)(2,1)S(1)}, bf16[128,2,1024]{2,0,1:T(8,128)(2,1)S(1)}, u32[]{:S(2)}, u32[]{:S(2)}) collective-permute-start(bf16[128,2,1024]{2,0,1:T(8,128)(2,1)S(1)} %convert_element_type.40), channel_id=1, source_target_pairs={{0,1},{1,2},{2,3},{3,4},{4,5},{5,6},{6,7},{8,9},{9,10},{10,11},{11... | collective-permute-start | bytes 1572872 | tf_op jit(solution)/shard_map/while/body/eval_jaxpr/ppermute | solution.py:11
  497.1 310.7 %copy-start = (bf16[128,1,2,1024]{3,2,1,0:T(2,128)(2,1)S(1)}, bf16[128,1,2,1024]{3,2,1,0:T(2,128)(2,1)}, u32[]{:S(2)}) copy-start(bf16[128,1,2,1024]{3,2,1,0:T(2,128)(2,1)} %param.19) | copy-start | bytes 1572868
  807.8 753.3 %copy-start.1 = (f32[128,2,128]{2,1,0:T(2,128)S(1)}, f32[128,2,128]{2,1,0:T(2,128)}, u32[]{:S(2)}) copy-start(f32[128,2,128]{2,1,0:T(2,128)} %param.18) | copy-start | bytes 393220
  809.1 752.1 %all-reduce.2.cloned.1.call-start = ((), (), s32[]{:S(2)}) async-start(), calls=%async_computation.3 | async-start | bytes 131072 | tf_op jit(solution)/shard_map/psum | solution.py:80
Sparse Core Ops, SparseCore 0:
  12.4 136.3 all-gather.4
  153.3 122.5 all-gather.2
  809.2 626.5 reduce-scatter.3
  1439.4 121.7 all-reduce.1
where the time goes:
time: 1570 us
  waiting for transfers between devices  1090 us (69%)
  local copies, waits for them, and re-layouts  332 us (21%)
  starting transfers between devices  124 us (8%)
    unnamed x5, waiting for transfers between devices  625 us
    gather x1, local copies, waits for them, and re-layouts, per_device(): values = jnp.take_along_axis(current, index_both, axis=2)  311 us
    all_gather x1, waiting for transfers between devices, per_device(): lax.all_gather(lower_inverse, 'src', axis=1, tiled=True)  137 us
    all_gather x1, waiting for transfers between devices, per_device(): lax.all_gather(coupling, 'src', axis=1, tiled=True)  127 us
    psum x1, waiting for transfers between devices, per_device(): picked = lax.psum(values.astype(jnp.bfloat16), 'fac').astype(jnp.float32)  124 us
    ppermute x8, starting transfers between devices, from_behind(): return lax.ppermute(shard, axis, pairs)  124 us
    ppermute x8, waiting for transfers between devices, from_behind(): return lax.ppermute(shard, axis, pairs)  73 us
  transfers between devices with their start and end apart: 12, of which 12 were waited for; matrix products, arithmetic and copies ran while one was open for 0% of the time, Pallas kernels for 0%

commit v1 on v0

--- a/solution.py
+++ b/solution.py
@@ -77,7 +77,7 @@
     index_both = jnp.broadcast_to(clipped[:, None, :], observed.shape)
     values = jnp.take_along_axis(current, index_both, axis=2)
     values = jnp.where(inside[:, None, :], values, jnp.zeros((), jnp.float32))
-    picked = lax.psum(values.astype(jnp.bfloat16), "fac").astype(jnp.float32)
+    picked = jnp.sum(lax.all_gather(values.astype(jnp.bfloat16), "fac"), axis=0).astype(jnp.float32)
     scale = 1.0 / math.sqrt(sources * lax.axis_size("src"))
     terms = jnp.sum(current * adjoint[:, 0].astype(jnp.float32), axis=(0, 1)) * scale
     gradient = lax.psum_scatter(terms[None, :], "src", scatter_dimension=1, tiled=True)

time: 1570 us -> 1510 us (0.962)
  the two profiles are of different devices: /device:TPU:2 before, /device:TPU:32 now
where the time goes in v1:
time: 1510 us; the launch traced here: 1500 us
  waiting for transfers between devices  931 us (62%)
  local copies, waits for them, and re-layouts  333 us (22%)
  blocking collectives  117 us (8%)
  starting transfers between devices  98.4 us (7%)
    unnamed x4, waiting for transfers between devices  566 us
    gather x1, local copies, waits for them, and re-layouts, per_device(): values = jnp.take_along_axis(current, index_both, axis=2)  311 us
    all_gather x1, waiting for transfers between devices, per_device(): lax.all_gather(lower_inverse, 'src', axis=1, tiled=True)  132 us
    all_gather x1, waiting for transfers between devices, per_device(): lax.all_gather(coupling, 'src', axis=1, tiled=True)  127 us
    all_gather x1, blocking collectives, per_device(): lax.all_gather(values.astype(jnp.bfloat16), 'fac')  117 us
    ppermute x8, waiting for transfers between devices, from_behind(): return lax.ppermute(shard, axis, pairs)  107 us
    ppermute x8, starting transfers between devices, from_behind(): return lax.ppermute(shard, axis, pairs)  98.3 us
  transfers between devices with their start and end apart: 11, of which 11 were waited for; matrix products, arithmetic and copies ran while one was open for 0% of the time, Pallas kernels for 0%

profile of v1, /device:TPU:32, one launch (start us, length us, event | category | flops | bytes accessed | tf_op | source)
XLA Modules:
  0.0 1504.8 jit_solution(6021189464388300669)
XLA Ops:
  11.8 131.5 %all-gather.5.cloned.1.call-done = bf16[1,1024,2,1024]{3,2,0,1:T(2,128)(2,1)} async-done(((bf16[1,16,2,1024]{3,2,0,1:T(2,128)(2,1)}), bf16[1,1024,2,1024]{3,2,0,1:T(2,128)(2,1)}) %all-gather.5.cloned.1.call-update) | async-done | bytes 4194320 | tf_op jit(solution)/shard_map/all_gather | solution.py:53
  143.3 127.0 %all-gather.3.cloned.1.call-done = bf16[1,1024,2,1024]{3,2,0,1:T(2,128)(2,1)} async-done(((bf16[1,16,2,1024]{3,2,0,1:T(2,128)(2,1)}), bf16[1,1024,2,1024]{3,2,0,1:T(2,128)(2,1)}) %all-gather.3.cloned.1.call-update) | async-done | bytes 4194320 | tf_op jit(solution)/shard_map/all_gather | solution.py:54
  270.4 229.8 %while.18 = (s32[]{:T(128)}, f32[128,2,1024]{2,0,1:T(8,128)S(1)}, bf16[128,2,1024]{2,0,1:T(8,128)(2,1)S(1)}, s32[]{:T(128)}, s32[128]{0:T(128)}, /*index=5*/f32[...) while((s32[]{:T(128)}, f32[128,2,1024]{2,0,1:T(8,128)S(1)}, ...), condition=%wide.region_3.4_spmd, body=%wide.region_0.3_spmd.sunk | while | flops 2154169344 | bytes 39597816 | solution.py:73
  272.6 42.2 %collective-permute-done = bf16[128,2,1024]{2,0,1:T(8,128)(2,1)S(1)} collective-permute-done((bf16[128,2,1024]{2,0,1:T(8,128)(2,1)S(1)}, bf16[128,2,1024]{2,0,1:T(8,128)(2,1)S(1)}, u32[]{:S(2)}, u32[]{:S(2)}) %collective-permute-start) | collective-permute-done | bytes 524320 | tf_op jit(solution)/shard_map/while/body/eval_jaxpr/ppermute | solution.py:11
  314.8 23.8 %conditional.2 = (f32[128,2,1024]{2,0,1:T(8,128)S(1)}) conditional(s32[]{:T(128)} %convert_element_type.48, f32[128,2,1024]{2,0,1:T(8,128)S(1)} %get-tuple-element.299, (s32[128]{0:T(128)}, s32[]{:T(128)}, f32[128,2]{0,1:T(2,128)}, bf16[128,2,1024]{2,0,1:T(8,128)(2,1)S(1)}, bf16[1,1024,2,1024]{3,2,1,0:T(2,128)(2,1)}, ...), branch_computations={%region_1.0_spmd, %region_2.2_spmd} | conditional | flops 2153907200 | bytes 35927604 | solution.py:69
  315.7 7.8 reshape.97
  323.6 3.5 fusion
  327.2 7.8 reshape.98
  340.5 13.6 collective-permute-done
  354.2 26.0 %collective-permute-start = (bf16[128,2,1024]{2,0,1:T(8,128)(2,1)S(1)}, bf16[128,2,1024]{2,0,1:T(8,128)(2,1)S(1)}, u32[]{:S(2)}, u32[]{:S(2)}) collective-permute-start(bf16[128,2,1024]{2,0,1:T(8,128)(2,1)S(1)} %convert_element_type.49), channel_id=1, source_target_pairs={{0,1},{1,2},{2,3},{3,4},{4,5},{5,6},{6,7},{8,9},{9,10},{10,11},{11... | collective-permute-start | bytes 1572872 | tf_op jit(solution)/shard_map/while/body/eval_jaxpr/ppermute | solution.py:11
  380.2 10.5 collective-permute-done
  390.8 4.4 collective-permute-start
  395.2 9.6 collective-permute-done
  404.8 26.2 %collective-permute-start = (bf16[128,2,1024]{2,0,1:T(8,128)(2,1)S(1)}, bf16[128,2,1024]{2,0,1:T(8,128)(2,1)S(1)}, u32[]{:S(2)}, u32[]{:S(2)}) collective-permute-start(bf16[128,2,1024]{2,0,1:T(8,128)(2,1)S(1)} %convert_element_type.49), channel_id=1, source_target_pairs={{0,1},{1,2},{2,3},{3,4},{4,5},{5,6},{6,7},{8,9},{9,10},{10,11},{11... | collective-permute-start | bytes 1572872 | tf_op jit(solution)/shard_map/while/body/eval_jaxpr/ppermute | solution.py:11
  431.1 9.0 collective-permute-done
  440.1 4.4 collective-permute-start
  444.5 8.0 collective-permute-done
  452.7 27.7 %collective-permute-start = (bf16[128,2,1024]{2,0,1:T(8,128)(2,1)S(1)}, bf16[128,2,1024]{2,0,1:T(8,128)(2,1)S(1)}, u32[]{:S(2)}, u32[]{:S(2)}) collective-permute-start(bf16[128,2,1024]{2,0,1:T(8,128)(2,1)S(1)} %convert_element_type.49), channel_id=1, source_target_pairs={{0,1},{1,2},{2,3},{3,4},{4,5},{5,6},{6,7},{8,9},{9,10},{10,11},{11... | collective-permute-start | bytes 1572872 | tf_op jit(solution)/shard_map/while/body/eval_jaxpr/ppermute | solution.py:11
  480.4 7.4 collective-permute-done
  487.9 5.6 collective-permute-start
  493.5 6.7 collective-permute-done
  500.2 310.7 %gather_fusion = bf16[32768]{0:T(1024)(128)(2,1)S(1)} fusion(f32[128,2,1024]{2,0,1:T(8,128)S(1)} %get-tuple-element.168, s32[32768]{0:T(1024)S(1)} %bitcast.37), kind=kCustom, calls=%fused_computation | custom fusion | bytes 524288 | tf_op jit(solution)/shard_map/jit(take_along_axis)/gather | solution.py:78
  811.4 117.3 %all_gather.12 = bf16[8,128,2,128]{3,1,2,0:T(8,128)(2,1)S(1)} all-gather(bf16[1,128,2,128]{3,1,2,0:T(8,128)(2,1)S(1)} %copy.38), channel_id=1, replica_groups=mesh['src'=64,'fac'=8] {'fac'}, dimensions={0}, use_global_device_ids=true | all-gather | bytes 589824 | tf_op jit(solution)/shard_map/all_gather | solution.py:80
  932.4 564.6 %reduce-scatter.4.cloned.1.call-done = f32[16,1]{1,0:T(8,128)} async-done(((f32[1024,1]{1,0:T(8,128)}), f32[16,1]{1,0:T(8,128)}) %reduce-scatter.4.cloned.1.call-update) | async-done | bytes 80
  (53 shorter events, 19.2 us)
Async XLA Ops:
  7.2 136.1 %all-gather.5.cloned.1.call-start = ((), (), s32[]{:S(2)}) async-start(), calls=%async_computation.2 | async-start | bytes 4259840 | tf_op jit(solution)/shard_map/all_gather | solution.py:53
  7.9 262.4 %all-gather.3.cloned.1.call-start = ((), (), s32[]{:S(2)}) async-start(), calls=%async_computation.1 | async-start | bytes 4259840 | tf_op jit(solution)/shard_map/all_gather | solution.py:54
  8.6 1488.4 %reduce-scatter.4.cloned.1.call-start = ((), (), s32[]{:S(2)}) async-start(), calls=%async_computation.3 | async-start | bytes 532480
  270.5 44.2 %collective-permute-start = (bf16[128,2,1024]{2,0,1:T(8,128)(2,1)S(1)}, bf16[128,2,1024]{2,0,1:T(8,128)(2,1)S(1)}, u32[]{:S(2)}, u32[]{:S(2)}) collective-permute-start(bf16[128,2,1024]{2,0,1:T(8,128)(2,1)S(1)} %convert_element_type.49), channel_id=1, source_target_pairs={{0,1},{1,2},{2,3},{3,4},{4,5},{5,6},{6,7},{8,9},{9,10},{10,11},{11... | collective-permute-start | bytes 1572872 | tf_op jit(solution)/shard_map/while/body/eval_jaxpr/ppermute | solution.py:11
  315.7 7.8 copy-start.2
  338.6 15.5 %collective-permute-start = (bf16[128,2,1024]{2,0,1:T(8,128)(2,1)S(1)}, bf16[128,2,1024]{2,0,1:T(8,128)(2,1)S(1)}, u32[]{:S(2)}, u32[]{:S(2)}) collective-permute-start(bf16[128,2,1024]{2,0,1:T(8,128)(2,1)S(1)} %convert_element_type.49), channel_id=1, source_target_pairs={{0,1},{1,2},{2,3},{3,4},{4,5},{5,6},{6,7},{8,9},{9,10},{10,11},{11... | collective-permute-start | bytes 1572872 | tf_op jit(solution)/shard_map/while/body/eval_jaxpr/ppermute | solution.py:11
  354.2 36.5 %collective-permute-start = (bf16[128,2,1024]{2,0,1:T(8,128)(2,1)S(1)}, bf16[128,2,1024]{2,0,1:T(8,128)(2,1)S(1)}, u32[]{:S(2)}, u32[]{:S(2)}) collective-permute-start(bf16[128,2,1024]{2,0,1:T(8,128)(2,1)S(1)} %convert_element_type.49), channel_id=1, source_target_pairs={{0,1},{1,2},{2,3},{3,4},{4,5},{5,6},{6,7},{8,9},{9,10},{10,11},{11... | collective-permute-start | bytes 1572872 | tf_op jit(solution)/shard_map/while/body/eval_jaxpr/ppermute | solution.py:11
  390.8 14.0 collective-permute-start
  404.8 35.2 %collective-permute-start = (bf16[128,2,1024]{2,0,1:T(8,128)(2,1)S(1)}, bf16[128,2,1024]{2,0,1:T(8,128)(2,1)S(1)}, u32[]{:S(2)}, u32[]{:S(2)}) collective-permute-start(bf16[128,2,1024]{2,0,1:T(8,128)(2,1)S(1)} %convert_element_type.49), channel_id=1, source_target_pairs={{0,1},{1,2},{2,3},{3,4},{4,5},{5,6},{6,7},{8,9},{9,10},{10,11},{11... | collective-permute-start | bytes 1572872 | tf_op jit(solution)/shard_map/while/body/eval_jaxpr/ppermute | solution.py:11
  440.1 12.4 collective-permute-start
  452.7 35.1 %collective-permute-start = (bf16[128,2,1024]{2,0,1:T(8,128)(2,1)S(1)}, bf16[128,2,1024]{2,0,1:T(8,128)(2,1)S(1)}, u32[]{:S(2)}, u32[]{:S(2)}) collective-permute-start(bf16[128,2,1024]{2,0,1:T(8,128)(2,1)S(1)} %convert_element_type.49), channel_id=1, source_target_pairs={{0,1},{1,2},{2,3},{3,4},{4,5},{5,6},{6,7},{8,9},{9,10},{10,11},{11... | collective-permute-start | bytes 1572872 | tf_op jit(solution)/shard_map/while/body/eval_jaxpr/ppermute | solution.py:11
  487.9 12.3 collective-permute-start
  500.2 311.0 %copy-start = (bf16[128,1,2,1024]{3,2,1,0:T(2,128)(2,1)S(1)}, bf16[128,1,2,1024]{3,2,1,0:T(2,128)(2,1)}, u32[]{:S(2)}) copy-start(bf16[128,1,2,1024]{3,2,1,0:T(2,128)(2,1)} %param.19) | copy-start | bytes 1572868
  810.9 119.0 %copy-start.1 = (f32[128,2,128]{2,1,0:T(2,128)S(1)}, f32[128,2,128]{2,1,0:T(2,128)}, u32[]{:S(2)}) copy-start(f32[128,2,128]{2,1,0:T(2,128)} %param.18) | copy-start | bytes 393220
Sparse Core Ops, SparseCore 0:
  12.4 130.8 all-gather.4
  147.7 122.5 all-gather.2
  929.9 567.1 reduce-scatter.3
